TPU v7x, 512 devices: a whole 4x8x8 slice. The times are simulated.
512 devices in a mesh: tile: 128 (over y, z_hi, x), head: 4 (over z_lo, core).
Axes of the slice: x: 4, y: 8, z: 8 (z_hi: 4, z_lo: 2; z = z_hi * 2 + z_lo), core: 2. Of those that a mesh axis runs over, the one named last changes fastest.
Arguments:
- queries: bfloat16 [32768, 1024], P('tile', 'head'), may hold values from -6 to 6
- keys: bfloat16 [32768, 1024], P('tile', 'head'), may hold values from -6 to 6
- values: bfloat16 [32768, 1024], P('tile', 'head'), may hold values from -6 to 6
- grad_output: bfloat16 [32768, 1024], P('tile', 'head'), may hold values from -24 to 24
- out_weight: bfloat16 [1024, 1024], P(None, 'head'), may hold values from -0.1875 to 0.1875
- rotations: int32 [128, 4], P('tile'), may hold values from 0 to 3, as said below
Outputs:
- grad_queries: bfloat16 [32768, 1024], P('tile', 'head')
- grad_keys: bfloat16 [32768, 1024], P('tile', 'head')
- grad_values: bfloat16 [32768, 1024], P('tile', 'head')
- grad_out_weight: float32 [1024, 1024], P('tile', 'head')
Inputs may be any that keep to these rules, and one draw needn't show every extreme that they name: The tiles form 4 rows of 32 in row-major order, grouped into faces of max(8, 2) whole columns; rotations[t, s] is 0 unless side s of tile t crosses a seam, that is an east or west side between two faces or a north or south side between the last and the first row. Across a seam the two facing sides hold r and (4 - r) mod 4 with r equal to 1 or 3.
All inputs are finite; a program needn't handle non-finite values.
Results may differ from a plain program's by a relative error of at most 0.012.
Values may be sent and summed in bfloat16 or wider, within the bound.
A program may use at most 64 MiB of HBM per device.

v0:
```python
import functools
import math

import jax
import jax.numpy as jnp
from jax import lax
from jax.sharding import PartitionSpec as P

HEAD_DIM = 64
RADIUS = 6
SIDE = 16


def for_sending(array):
    return jax.tree.map(lambda a: a.astype(jnp.bfloat16) if a.dtype == jnp.float32 else a, array)


def from_behind(block, axis, distance):
    devices = range(lax.axis_size(axis))
    route = [((i - distance) % len(devices), i) for i in devices]
    return lax.ppermute(block, axis, route)


def turned_rim(tile_grid, number):
    return jnp.rot90(tile_grid, number)[tile_grid.shape[0] - RADIUS :]


def placed_back(strip, number, tile_side):
    padded = jnp.pad(strip, ((tile_side - RADIUS, 0), (0, 0), (0, 0)))
    return jnp.rot90(padded, -number)


def place_back(strip, turn_count, tile_side):
    branches = [
        functools.partial(placed_back, number=number, tile_side=tile_side) for number in range(4)
    ]
    return lax.switch(turn_count, branches, strip)


def extend(tile_grid, strips):
    tile_side = tile_grid.shape[0]
    extended = jnp.pad(tile_grid, ((RADIUS, RADIUS), (RADIUS, RADIUS), (0, 0)))
    for side_index in range(4):
        turned = jnp.rot90(extended, side_index)
        turned = turned.at[:RADIUS, RADIUS : RADIUS + tile_side].set(strips[side_index])
        extended = jnp.rot90(turned, -side_index)
    return extended


def inner_rim(extended, side_index, tile_side):
    return jnp.rot90(extended, side_index)[:RADIUS, RADIUS : RADIUS + tile_side]


def window_backward(query_grid, key_ext, value_ext, dout_grid):
    tile_side = query_grid.shape[0]
    features = query_grid.shape[-1]
    extended = tile_side + 2 * RADIUS
    score_scale = HEAD_DIM ** (-0.5)
    query_rows = query_grid.reshape(tile_side * tile_side, features)
    dout_rows = dout_grid.reshape(tile_side * tile_side, features)
    key_rows = key_ext.reshape(extended * extended, features)
    value_rows = value_ext.reshape(extended * extended, features)
    query_index = jnp.arange(tile_side * tile_side, dtype=jnp.int32)
    query_row = query_index // tile_side + RADIUS
    query_col = query_index % tile_side + RADIUS
    cell_index = jnp.arange(extended * extended, dtype=jnp.int32)
    cell_row = cell_index // extended
    cell_col = cell_index % extended
    outer_row = (cell_row < RADIUS) | (cell_row >= RADIUS + tile_side)
    outer_col = (cell_col < RADIUS) | (cell_col >= RADIUS + tile_side)
    corner = outer_row & outer_col
    allowed = (
        (jnp.abs(cell_row[None, :] - query_row[:, None]) <= RADIUS)
        & (jnp.abs(cell_col[None, :] - query_col[:, None]) <= RADIUS)
        & jnp.logical_not(corner)[None, :]
    )
    attention_list = []
    grad_query_list = []
    grad_key_list = []
    grad_value_list = []
    for head_index in range(features // HEAD_DIM):
        head_cols = slice(head_index * HEAD_DIM, (head_index + 1) * HEAD_DIM)
        query_head = query_rows[:, head_cols]
        key_head = key_rows[:, head_cols]
        value_head = value_rows[:, head_cols]
        dout_head = dout_rows[:, head_cols]
        scores = (
            lax.dot_general(
                query_head, key_head, (((1,), (1,)), ((), ())), preferred_element_type=jnp.float32
            )
            * score_scale
        )
        scores = jnp.where(allowed, scores, -1e30)
        row_max = jnp.max(scores, axis=1, keepdims=True)
        raw_weights = jnp.exp(scores - row_max)
        weights = raw_weights / jnp.sum(raw_weights, axis=1, keepdims=True)
        weights_bf = weights.astype(jnp.bfloat16)
        attention = jnp.dot(weights_bf, value_head, preferred_element_type=jnp.float32)
        row_delta = jnp.sum(dout_head.astype(jnp.float32) * attention, axis=1, keepdims=True)
        grad_weights = lax.dot_general(
            dout_head, value_head, (((1,), (1,)), ((), ())), preferred_element_type=jnp.float32
        )
        dscore = (weights * (grad_weights - row_delta)).astype(jnp.bfloat16)
        grad_query = jnp.dot(dscore, key_head, preferred_element_type=jnp.float32) * score_scale
        grad_key = (
            lax.dot_general(
                dscore, query_head, (((0,), (0,)), ((), ())), preferred_element_type=jnp.float32
            )
            * score_scale
        )
        grad_value = lax.dot_general(
            weights_bf, dout_head, (((0,), (0,)), ((), ())), preferred_element_type=jnp.float32
        )
        attention_list.append(attention)
        grad_query_list.append(grad_query)
        grad_key_list.append(grad_key)
        grad_value_list.append(grad_value)
    attention_all = jnp.concatenate(attention_list, axis=1)
    grad_query_all = jnp.concatenate(grad_query_list, axis=1)
    grad_key_all = jnp.concatenate(grad_key_list, axis=1).reshape(extended, extended, features)
    grad_value_all = jnp.concatenate(grad_value_list, axis=1).reshape(extended, extended, features)
    return (attention_all, grad_query_all, grad_key_all, grad_value_all)


def shards(queries, keys, values, grad_output, out_weight, rotations):
    tile_count = lax.axis_size("tile")
    token_count = queries.shape[0]
    features = queries.shape[1]
    tile_side = SIDE
    full_cotangent = lax.all_gather(grad_output, "head", axis=1, tiled=True)
    dout = jnp.dot(full_cotangent, out_weight, preferred_element_type=jnp.float32).astype(
        jnp.bfloat16
    )
    tile_grid = jnp.concatenate([keys, values], axis=1).reshape(tile_side, tile_side, 2 * features)
    offsets = (-(tile_count // 4), 1, tile_count // 4, -1)
    strips = []
    all_edges = jnp.stack([turned_rim(tile_grid, number) for number in range(4)])
    for side_index in range(4):
        arrived = from_behind(for_sending(all_edges), "tile", -offsets[side_index]).astype(
            all_edges.dtype
        )
        turn_count = (side_index + rotations[0, side_index]) % 4
        strips.append(lax.dynamic_index_in_dim(arrived, turn_count, 0, keepdims=False))
    extended = extend(tile_grid, strips)
    attention, grad_query, grad_key, grad_value = window_backward(
        queries.reshape(tile_side, tile_side, features),
        extended[..., :features],
        extended[..., features:],
        dout.reshape(tile_side, tile_side, features),
    )
    grad_pair = jnp.concatenate([grad_key, grad_value], axis=-1)
    total = grad_pair[RADIUS : RADIUS + tile_side, RADIUS : RADIUS + tile_side]
    for side_index in range(4):
        sent_turn = ((side_index + rotations[0, side_index]) % 4).astype(jnp.float32).reshape(1)
        returned, returned_turn = from_behind(
            (inner_rim(grad_pair, side_index, tile_side), sent_turn), "tile", offsets[side_index]
        )
        total = total + place_back(returned, returned_turn[0].astype(jnp.int32), tile_side)
    grad_keys = total[..., :features].reshape(token_count, features).astype(jnp.bfloat16)
    grad_values = total[..., features:].reshape(token_count, features).astype(jnp.bfloat16)
    grad_queries = grad_query.astype(jnp.bfloat16)
    attention_bf = attention.astype(jnp.bfloat16)
    summed = lax.psum_scatter(
        lax.dot_general(
            full_cotangent,
            attention_bf,
            (((0,), (0,)), ((), ())),
            preferred_element_type=jnp.float32,
        ),
        "tile",
        scatter_dimension=0,
        tiled=True,
    )
    grad_out_weight = summed * (1.0 / math.sqrt(token_count * tile_count))
    return (grad_queries, grad_keys, grad_values, grad_out_weight)


def solution(mesh):
    placed = (
        P("tile", "head"),
        P("tile", "head"),
        P("tile", "head"),
        P("tile", "head"),
        P(None, "head"),
        P("tile", None),
    )
    return jax.shard_map(
        shards,
        mesh=mesh,
        in_specs=placed,
        out_specs=(P("tile", "head"), P("tile", "head"), P("tile", "head"), P("tile", "head")),
        check_vma=False,
    )
```

profile of v0, /device:TPU:32, one launch (start us, length us, event | category | flops | bytes accessed | tf_op | source)
XLA Modules:
  0.0 909.8 jit_solution(2949230822616872619)
XLA Ops:
  10.9 3.4 collective-permute-start.3
  14.3 2.2 collective-permute-start.2
  16.5 11.5 %collective-permute-start.1 = (bf16[4,6,16,512]{3,1,2,0:T(8,128)(2,1)}, bf16[4,6,16,512]{3,1,2,0:T(8,128)(2,1)}, u32[]{:S(2)}, u32[]{:S(2)}) collective-permute-start(bf16[4,6,16,512]{3,1,2,0:T(8,128)(2,1)} %pad_maximum_fusion.2), channel_id=1, source_target_pairs={{4,0},{8,4},{12,8},{16,12},{20,16},{24,20},{28,24},{32,28},{36,32}... | collective-permute-start | bytes 1179656 | tf_op jit(solution)/shard_map/ppermute | solution.py:21
  28.1 4.5 collective-permute-start
  33.9 22.6 %collective-permute-start.10 = (f32[1]{0:T(128)}, f32[1]{0:T(128)}, u32[]{:S(2)}, u32[]{:S(2)}) collective-permute-start(f32[1]{0:T(128)} %bitcast.42), channel_id=1, source_target_pairs={{4,0},{8,4},{12,8},{16,12},{20,16},{24,20},{28,24},{32,28},{36,32}... | collective-permute-start | bytes 20 | tf_op jit(solution)/shard_map/ppermute | solution.py:21
  56.5 9.8 %all_gather.3 = bf16[256,1024]{1,0:T(8,128)(2,1)S(1)} all-gather(bf16[256,256]{1,0:T(8,128)(2,1)S(1)} %copy-done.21), channel_id=1, replica_groups=mesh['tile'=128,'head'=4] {'head'}, dimensions={1}, use_global_device_ids=true | all-gather | bytes 655360 | tf_op jit(solution)/shard_map/all_gather | solution.py:130
  68.6 1.4 pad_dynamic-slice_fusion
  73.4 3.2 collective-permute-start.6
  77.3 7.9 collective-permute-done.6
  85.2 3.2 collective-permute-start.4
  89.0 2.6 collective-permute-done.4
  91.6 6.5 collective-permute-start.8
  100.6 1.6 scatter.14
  103.3 2.8 bitcast_select_fusion.1
  106.1 1.7 scatter.15
  108.8 1.9 bitcast_select_fusion.2
  110.8 1.6 scatter.16
  112.4 2.1 rev.101
  114.5 1.2 rev.102
  115.7 2.8 bitcast_select_fusion
  118.6 1.7 scatter.19
  121.9 1.9 fusion.105
  129.7 1.2 copy.113
  131.2 1.5 fusion.15
  133.0 1.1 copy-done.5
  137.0 1.2 copy.112
  138.2 1.3 reshape.281
  140.9 1.3 copy.131
  142.3 1.3 constant_dynamic-update-slice_fusion.2
  143.6 2.2 rev.104
  146.5 2.3 collective-permute-start.11
  149.6 1.3 slice.262
  151.0 4.0 collective-permute-start.9
  155.0 3.9 collective-permute-start.5
  158.9 1.7 slice.287
  160.6 3.5 collective-permute-start.7
  164.1 1.3 fusion.16
  165.4 1.4 fusion.17
  166.8 1.3 fusion.18
  168.1 1.4 fusion.19
  170.3 5.7 conditional.7
  171.2 3.2 rev.90
  174.4 1.3 copy.148
  177.7 3.0 conditional.6
  177.8 1.5 rev.86
  179.3 1.4 copy.143
  182.5 1.8 fusion.33
  185.0 716.4 %reduce-scatter.4.cloned.1.call-done = f32[8,256]{1,0:T(8,128)} async-done(((f32[1024,256]{1,0:T(8,128)}), f32[8,256]{1,0:T(8,128)}) %reduce-scatter.4.cloned.1.call-update) | async-done | bytes 8208
  (136 shorter events, 32.1 us)
Async XLA Ops:
  7.2 59.1 %copy-start = (bf16[1024,256]{1,0:T(8,128)(2,1)S(1)}, bf16[1024,256]{1,0:T(8,128)(2,1)}, u32[]{:S(2)}) copy-start(bf16[1024,256]{1,0:T(8,128)(2,1)} %param.34) | copy-start | bytes 1572868
  7.2 894.3 %reduce-scatter.4.cloned.1.call-start = ((), (), s32[]{:S(2)}) async-start(), calls=%async_computation.1 | async-start | bytes 1056768
  8.2 24.4 %copy-start.22 = (s32[1,4]{1,0:T(1,128)S(1)}, s32[1,4]{1,0:T(1,128)}, u32[]{:S(2)}) copy-start(s32[1,4]{1,0:T(1,128)} %param.35) | copy-start | bytes 52
  8.2 48.3 %copy-start.21 = (bf16[256,256]{1,0:T(8,128)(2,1)S(1)}, bf16[256,256]{1,0:T(8,128)(2,1)}, u32[]{:S(2)}) copy-start(bf16[256,256]{1,0:T(8,128)(2,1)} %param.33) | copy-start | bytes 393220
  9.9 57.4 %copy-start.23 = (s32[3]{0:T(128)S(1)}, s32[3]{0:T(128)}, u32[]{:S(2)}) copy-start(s32[3]{0:T(128)} %constant.253.clone.1) | copy-start | bytes 40
  10.9 104.8 %collective-permute-start.3 = (bf16[4,6,16,512]{3,1,2,0:T(8,128)(2,1)}, bf16[4,6,16,512]{3,1,2,0:T(8,128)(2,1)}, u32[]{:S(2)}, u32[]{:S(2)}) collective-permute-start(bf16[4,6,16,512]{3,1,2,0:T(8,128)(2,1)} %pad_maximum_fusion.2), channel_id=1, source_target_pairs={{508,0},{0,4},{4,8},{8,12},{12,16},{16,20},{20,24},{24,28},{28,32}... | collective-permute-start | bytes 1179656 | tf_op jit(solution)/shard_map/ppermute | solution.py:21
  14.3 93.6 %collective-permute-start.2 = (bf16[4,6,16,512]{3,1,2,0:T(8,128)(2,1)}, bf16[4,6,16,512]{3,1,2,0:T(8,128)(2,1)}, u32[]{:S(2)}, u32[]{:S(2)}) collective-permute-start(bf16[4,6,16,512]{3,1,2,0:T(8,128)(2,1)} %pad_maximum_fusion.2), channel_id=1, source_target_pairs={{128,0},{132,4},{136,8},{140,12},{144,16},{148,20},{152,24},{156,2... | collective-permute-start | bytes 1179656 | tf_op jit(solution)/shard_map/ppermute | solution.py:21
  16.5 86.7 %collective-permute-start.1 = (bf16[4,6,16,512]{3,1,2,0:T(8,128)(2,1)}, bf16[4,6,16,512]{3,1,2,0:T(8,128)(2,1)}, u32[]{:S(2)}, u32[]{:S(2)}) collective-permute-start(bf16[4,6,16,512]{3,1,2,0:T(8,128)(2,1)} %pad_maximum_fusion.2), channel_id=1, source_target_pairs={{4,0},{8,4},{12,8},{16,12},{20,16},{24,20},{28,24},{32,28},{36,32}... | collective-permute-start | bytes 1179656 | tf_op jit(solution)/shard_map/ppermute | solution.py:21
  28.1 71.8 %collective-permute-start = (bf16[4,6,16,512]{3,1,2,0:T(8,128)(2,1)}, bf16[4,6,16,512]{3,1,2,0:T(8,128)(2,1)S(1)}, u32[]{:S(2)}, u32[]{:S(2)}) collective-permute-start(bf16[4,6,16,512]{3,1,2,0:T(8,128)(2,1)} %pad_maximum_fusion.2), channel_id=1, source_target_pairs={{384,0},{388,4},{392,8},{396,12},{400,16},{404,20},{408,24},{412,2... | collective-permute-start | bytes 1179656 | tf_op jit(solution)/shard_map/ppermute | solution.py:21
  33.9 39.6 %collective-permute-start.10 = (f32[1]{0:T(128)}, f32[1]{0:T(128)}, u32[]{:S(2)}, u32[]{:S(2)}) collective-permute-start(f32[1]{0:T(128)} %bitcast.42), channel_id=1, source_target_pairs={{4,0},{8,4},{12,8},{16,12},{20,16},{24,20},{28,24},{32,28},{36,32}... | collective-permute-start | bytes 20 | tf_op jit(solution)/shard_map/ppermute | solution.py:21
  73.4 11.7 %collective-permute-start.6 = (f32[1]{0:T(128)}, f32[1]{0:T(128)}, u32[]{:S(2)}, u32[]{:S(2)}) collective-permute-start(f32[1]{0:T(128)} %bitcast.37), channel_id=1, source_target_pairs={{508,0},{0,4},{4,8},{8,12},{12,16},{16,20},{20,24},{24,28},{28,32}... | collective-permute-start | bytes 20 | tf_op jit(solution)/shard_map/ppermute | solution.py:21
  85.2 6.5 collective-permute-start.4
  91.6 7.7 collective-permute-start.8
  120.3 1.0 copy-start.13
  120.6 0.7 copy-start.19
  121.9 2.2 copy-start.3
  123.9 1.6 copy-start.1
  124.0 1.1 copy-start.12
  125.3 0.9 copy-start.14
  125.3 1.1 copy-start.20
  127.0 1.5 copy-start.4
  128.5 0.9 copy-start.6
  131.2 1.6 copy-start.2
  132.7 3.5 copy-start.15
  132.7 1.4 copy-start.5
  133.0 3.6 copy-start.16
  134.2 1.1 copy-start.7
  134.5 1.4 copy-start.17
  135.6 1.0 copy-start.18
  138.2 1.4 copy-start.8
  146.5 23.7 %collective-permute-start.11 = (f32[6,16,512]{2,0,1:T(8,128)}, f32[6,16,512]{2,0,1:T(8,128)S(1)}, u32[]{:S(2)}, u32[]{:S(2)}) collective-permute-start(f32[6,16,512]{2,0,1:T(8,128)} %slice.264), channel_id=1, source_target_pairs={{4,0},{8,4},{12,8},{16,12},{20,16},{24,20},{28,24},{32,28},{36,32}... | collective-permute-start | bytes 589832 | tf_op jit(solution)/shard_map/ppermute | solution.py:21
  151.0 25.9 %collective-permute-start.9 = (f32[6,16,512]{2,1,0:T(8,128)}, f32[6,16,512]{2,1,0:T(8,128)S(1)}, u32[]{:S(2)}, u32[]{:S(2)}) collective-permute-start(f32[6,16,512]{2,1,0:T(8,128)} %slice.262), channel_id=1, source_target_pairs={{384,0},{388,4},{392,8},{396,12},{400,16},{404,20},{408,24},{412,2... | collective-permute-start | bytes 589832 | tf_op jit(solution)/shard_map/ppermute | solution.py:21
  155.0 21.0 %collective-permute-start.5 = (f32[6,16,512]{2,1,0:T(8,128)}, f32[6,16,512]{2,1,0:T(8,128)S(1)}, u32[]{:S(2)}, u32[]{:S(2)}) collective-permute-start(f32[6,16,512]{2,1,0:T(8,128)} %get-tuple-element.116), channel_id=1, source_target_pairs={{128,0},{132,4},{136,8},{140,12},{144,16},{148,20},{152,24},{156,2... | collective-permute-start | bytes 589832 | tf_op jit(solution)/shard_map/ppermute | solution.py:21
  160.6 20.1 %collective-permute-start.7 = (f32[6,16,512]{2,0,1:T(8,128)}, f32[6,16,512]{2,0,1:T(8,128)S(1)}, u32[]{:S(2)}, u32[]{:S(2)}) collective-permute-start(f32[6,16,512]{2,0,1:T(8,128)} %slice.287), channel_id=1, source_target_pairs={{508,0},{0,4},{4,8},{8,12},{12,16},{16,20},{20,24},{24,28},{28,32}... | collective-permute-start | bytes 589832 | tf_op jit(solution)/shard_map/ppermute | solution.py:21
  176.0 0.8 copy-start.9
  176.8 0.8 copy-start.10
  180.7 0.8 copy-start.11
Sparse Core Ops, SparseCore 0:
  142.3 759.0 reduce-scatter.3
where the time goes:
time: 911 us; the launch traced here: 910 us
  waiting for transfers between devices  728 us (80%)
  starting transfers between devices  71 us (8%)
  local copies, waits for them, and re-layouts  50.5 us (6%)
  between operations  21.2 us (2%)
  matrix products  16.3 us (2%)
  other arithmetic  13.2 us (1%)
  blocking collectives  9.76 us (1%)
    unnamed x2, waiting for transfers between devices  716 us
    ppermute x12, starting transfers between devices, from_behind(): return lax.ppermute(block, axis, route)  70.9 us
  transfers between devices with their start and end apart: 13, of which 4 were waited for; matrix products, arithmetic and copies ran while one was open for 5% of the time, Pallas kernels for 0%

commit v1 on v0

v1 whole, which is shorter than its diff:
```python
import functools
import math

import jax
import jax.numpy as jnp
from jax import lax
from jax.experimental import pallas as pl
from jax.experimental.pallas import tpu as pltpu
from jax.sharding import PartitionSpec as P

HEAD_DIM = 64
RADIUS = 6
SIDE = 16
CELLS = SIDE * SIDE
STRIP = RADIUS * SIDE
EXT = CELLS + 4 * STRIP
MESH = pl.DeviceIdType.MESH
BF = jnp.bfloat16
F32 = jnp.float32
NT = (((1,), (1,)), ((), ()))


def dot(a, b):
    return jnp.dot(a, b, preferred_element_type=F32)


def dot_nt(a, b):
    return lax.dot_general(a, b, NT, preferred_element_type=F32)


def tile_axes(tile_count):
    return {128: (8, 4, 4), 8: (2, 2, 2)}[tile_count]


def kernel(
    tile_count,
    q_hbm,
    k_hbm,
    v_hbm,
    g_hbm,
    w_hbm,
    rot_ref,
    gq_hbm,
    gk_hbm,
    gv_hbm,
    gow_hbm,
    qbuf,
    kv,
    gbuf,
    gturned,
    wbuf,
    pick,
    pick_turned,
    strips,
    bias,
    qstack,
    kvt,
    weights,
    weights_bf,
    dscore,
    att_t,
    dstack,
    dturned,
    centre,
    back,
    returned,
    xsend,
    xrecv,
    ysum,
    yrecv,
    zsum,
    zrecv,
    gq_out,
    gkv_out,
    gow_out,
    gq_t,
    load_sem,
    store_sem,
    ag_send,
    ag_recv,
    halo_send,
    halo_recv,
    ret_send,
    ret_recv,
    x_send,
    x_recv,
    y_send,
    y_recv,
    z_send,
    z_recv,
):
    ny, nz, nx = tile_axes(tile_count)
    features = q_hbm.shape[1]
    heads = features // HEAD_DIM
    rows = gow_hbm.shape[0]
    t = lax.axis_index("tile")
    h = lax.axis_index("head")
    x = lax.rem(t, nx)
    z = lax.rem(t // nx, nz)
    y = t // (nx * nz)
    h1 = h + 1 - 2 * lax.rem(h, 2)
    h2 = lax.rem(h + 2, 4)
    h3 = 3 - h

    def at_xyz(yy, zz, xx):
        return (yy * nz + zz) * nx + xx

    def x_peer(k):
        return at_xyz(y, z, lax.rem(x + k, nx))

    def y_peer(k):
        return at_xyz(lax.rem(y + k, ny), z, x)

    def z_peer(k):
        return at_xyz(y, lax.rem(z + k, nz), x)

    offsets = (-(tile_count // 4), 1, tile_count // 4, -1)

    def beside(side):
        return lax.rem(t + offsets[side] + tile_count, tile_count)

    loads = [
        pltpu.make_async_copy(k_hbm, kv.at[0:CELLS, 0:features], load_sem.at[0]),
        pltpu.make_async_copy(v_hbm, kv.at[0:CELLS, features : 2 * features], load_sem.at[1]),
        pltpu.make_async_copy(q_hbm, qbuf, load_sem.at[2]),
        pltpu.make_async_copy(g_hbm, gbuf.at[0], load_sem.at[3]),
        pltpu.make_async_copy(w_hbm, wbuf, load_sem.at[4]),
    ]
    barrier = pltpu.get_barrier_semaphore()
    peers = [(t, h1), (t, h2), (t, h3)]
    peers += [(beside(side), h) for side in range(4)]
    peers += [(y_peer(k), h) for k in range(1, ny)]
    peers += [(x_peer(k), h) for k in range(1, nx)]
    peers += [(z_peer(k), h) for k in range(1, nz)]
    for peer in peers:
        pl.semaphore_signal(barrier, inc=1, device_id=peer, device_id_type=MESH)
    for load in loads:
        load.start()

    starts, down, along = [], [], []
    for side in range(4):
        turn = lax.rem(side + 4 - rot_ref[0, (side + 2) % 4], 4)

        def choose(a, b, c, d, turn=turn):
            return jnp.where(turn == 0, a, jnp.where(turn == 1, b, jnp.where(turn == 2, c, d)))

        starts.append(choose(160, 5, 95, 250))
        down.append(choose(16, -1, -16, 1))
        along.append(choose(1, 16, -1, -16))
    place = lax.broadcasted_iota(jnp.int32, (STRIP, CELLS), 0)
    cell = lax.broadcasted_iota(jnp.int32, (STRIP, CELLS), 1)
    for side in range(4):
        target = starts[side] + down[side] * (place // SIDE) + along[side] * (place % SIDE)
        pick[side * STRIP : (side + 1) * STRIP, :] = jnp.where(cell == target, 1.0, 0.0).astype(BF)
    loads[0].wait()
    loads[1].wait()
    strips[...] = dot(pick[...], kv[0:CELLS, :]).astype(BF)

    halos = [
        pltpu.make_async_remote_copy(
            src_ref=strips.at[side * STRIP : (side + 1) * STRIP],
            dst_ref=kv.at[CELLS + side * STRIP : CELLS + (side + 1) * STRIP],
            send_sem=halo_send.at[side],
            recv_sem=halo_recv.at[side],
            device_id=(beside((side + 2) % 4), h),
            device_id_type=MESH,
        )
        for side in range(4)
    ]
    gathers = [
        pltpu.make_async_remote_copy(
            src_ref=source,
            dst_ref=gbuf.at[slot],
            send_sem=ag_send.at[slot - 1],
            recv_sem=ag_recv.at[slot - 1],
            device_id=(t, peer),
            device_id_type=MESH,
        )
        for slot, source, peer in ((1, g_hbm, h1), (2, g_hbm, h2), (3, gbuf.at[2], h1))
    ]
    pl.semaphore_wait(barrier, len(peers))
    for halo in halos:
        halo.start()
    gathers[1].start()
    gathers[0].start()

    cell_t = lax.broadcasted_iota(jnp.int32, (CELLS, 4 * STRIP), 0)
    place_t = lax.broadcasted_iota(jnp.int32, (CELLS, 4 * STRIP), 1)
    side_t = place_t // STRIP
    rest_t = place_t - side_t * STRIP

    def by_side(values):
        return jnp.where(
            side_t == 0,
            values[0],
            jnp.where(side_t == 1, values[1], jnp.where(side_t == 2, values[2], values[3])),
        )

    target_t = by_side(starts) + by_side(down) * (rest_t // SIDE) + by_side(along) * (rest_t % SIDE)
    pick_turned[...] = jnp.where(cell_t == target_t, 1.0, 0.0).astype(BF)

    def fill_bias(first, count, where_is):
        index = lax.broadcasted_iota(jnp.int32, (count, CELLS), 0)
        query = lax.broadcasted_iota(jnp.int32, (count, CELLS), 1)
        a, b = where_is(index // SIDE, index % SIDE)
        off_a = a - query // SIDE
        off_b = b - query % SIDE
        inside = (off_a >= 0) & (off_a <= 2 * RADIUS) & (off_b >= 0) & (off_b <= 2 * RADIUS)
        bias[first : first + count, :] = jnp.where(inside, 0.0, -1e30)

    last = SIDE + 2 * RADIUS - 1
    fill_bias(0, CELLS, lambda i, j: (i + RADIUS, j + RADIUS))
    fill_bias(CELLS, STRIP, lambda i, j: (i, RADIUS + j))
    fill_bias(CELLS + STRIP, STRIP, lambda i, j: (RADIUS + j, last - i))
    fill_bias(CELLS + 2 * STRIP, STRIP, lambda i, j: (last - i, last - RADIUS - j))
    fill_bias(CELLS + 3 * STRIP, STRIP, lambda i, j: (last - RADIUS - j, i))

    loads[2].wait()
    lane = lax.broadcasted_iota(jnp.int32, (CELLS, features), 1)
    scaled = qbuf[...].astype(F32) * (HEAD_DIM ** (-0.5))
    for head in range(heads):
        own = lane // HEAD_DIM == head
        qstack[head * CELLS : (head + 1) * CELLS, :] = jnp.where(own, scaled, 0.0).astype(BF)

    gathers[1].wait_recv()
    gathers[2].start()
    loads[3].wait()
    gturned[0] = gbuf[0].T
    gturned[2] = gbuf[2].T
    gathers[0].wait_recv()
    gturned[1] = gbuf[1].T
    for halo in halos:
        halo.wait_recv()
    kvt[...] = kv[...].T
    gathers[2].wait_recv()
    gturned[3] = gbuf[3].T

    pieces = 5
    piece = EXT // pieces
    for head in range(heads):
        cols = slice(head * CELLS, (head + 1) * CELLS)
        score = dot_nt(kv[:, 0:features], qstack[cols, :])
        top = None
        for n in range(pieces):
            part = slice(n * piece, (n + 1) * piece)
            masked = score[part] + bias[part, :]
            weights[part, cols] = masked
            highest = jnp.max(masked.reshape(piece // 8, 8, CELLS), axis=0)
            top = highest if top is None else jnp.maximum(top, highest)
        top = jnp.max(top, axis=0, keepdims=True)
        total = None
        for n in range(pieces):
            part = slice(n * piece, (n + 1) * piece)
            raw = jnp.exp(weights[part, cols] - top)
            weights[part, cols] = raw
            summed = jnp.sum(raw.reshape(piece // 8, 8, CELLS), axis=0)
            total = summed if total is None else total + summed
        inverse = 1.0 / jnp.sum(total, axis=0, keepdims=True)
        for n in range(pieces):
            part = slice(n * piece, (n + 1) * piece)
            normal = weights[part, cols] * inverse
            weights[part, cols] = normal
            weights_bf[part, cols] = normal.astype(BF)
        own_rows = slice(head * HEAD_DIM, (head + 1) * HEAD_DIM)
        att_t[own_rows, :] = dot(
            kvt[features + head * HEAD_DIM : features + (head + 1) * HEAD_DIM, :],
            weights_bf[:, cols],
        )
    att_bf = att_t[...].astype(BF)

    holders = (h, h1, h2, h3)
    per_slot = features // rows // nx * rows
    for slot in range(4):
        term = dot_nt(gturned[slot], att_bf)
        term = term.reshape(per_slot // rows, nx, rows, features)
        for xx in range(nx):
            first = pl.multiple_of(holders[slot] * per_slot, per_slot)
            xsend[xx, pl.ds(first, per_slot), :] = (
                term[:, xx].reshape(per_slot, features).astype(BF)
            )
    x_copies = [
        pltpu.make_async_remote_copy(
            src_ref=xsend.at[lax.rem(x + k, nx)],
            dst_ref=xrecv.at[k - 1],
            send_sem=x_send.at[k - 1],
            recv_sem=x_recv.at[k - 1],
            device_id=(x_peer(k), h),
            device_id_type=MESH,
        )
        for k in range(1, nx)
    ]
    for copy in x_copies:
        copy.start()

    loads[4].wait()
    dout = None
    for slot in range(4):
        first = pl.multiple_of(holders[slot] * features, features)
        term = dot(gbuf[slot], wbuf[pl.ds(first, features), :])
        dout = term if dout is None else dout + term
    dout_bf = dout.astype(BF)
    dout = dout_bf.astype(F32)
    dout_t = dout.T
    row = lax.broadcasted_iota(jnp.int32, (features, CELLS), 0)
    product = dout_t * att_t[...]
    for head in range(heads):
        own = lane // HEAD_DIM == head
        dstack[head * CELLS : (head + 1) * CELLS, :] = jnp.where(own, dout, 0.0).astype(BF)
        own = row // HEAD_DIM == head
        dturned[head * features : (head + 1) * features, :] = jnp.where(own, dout_t, 0.0).astype(BF)
    for head in range(heads):
        cols = slice(head * CELLS, (head + 1) * CELLS)
        own_rows = slice(head * HEAD_DIM, (head + 1) * HEAD_DIM)
        delta = jnp.sum(product[own_rows], axis=0, keepdims=True)
        grad_weight = dot(kv[:, features : 2 * features], dturned[head * features : (head + 1) * features, :])
        for n in range(pieces):
            part = slice(n * piece, (n + 1) * piece)
            dscore[part, cols] = (weights[part, cols] * (grad_weight[part] - delta)).astype(BF)
        gq_t[own_rows, :] = dot(kvt[own_rows, :], dscore[:, cols])
    back[:, 0:features] = dot(dscore[CELLS:EXT, :], qstack[...]).astype(BF)
    back[:, features : 2 * features] = dot(weights_bf[CELLS:EXT, :], dstack[...]).astype(BF)
    returns = [
        pltpu.make_async_remote_copy(
            src_ref=back.at[side * STRIP : (side + 1) * STRIP],
            dst_ref=returned.at[side * STRIP : (side + 1) * STRIP],
            send_sem=ret_send.at[side],
            recv_sem=ret_recv.at[side],
            device_id=(beside(side), h),
            device_id_type=MESH,
        )
        for side in range(4)
    ]
    for copy in returns:
        copy.start()
    centre[:, 0:features] = dot(dscore[0:CELLS, :], qstack[...])
    centre[:, features : 2 * features] = dot(weights_bf[0:CELLS, :], dstack[...])
    gq_out[...] = (gq_t[...].T * (HEAD_DIM ** (-0.5))).astype(BF)
    stores = [pltpu.make_async_copy(gq_out, gq_hbm, store_sem.at[0])]
    stores[0].start()

    for copy in x_copies:
        copy.wait_recv()
    total = xsend[x].astype(F32)
    for k in range(nx - 1):
        total = total + xrecv[k].astype(F32)
    ysum[...] = total.astype(BF)
    block = nz * rows
    y_copies = [
        pltpu.make_async_remote_copy(
            src_ref=ysum.at[pl.ds(pl.multiple_of(lax.rem(y + k, ny) * block, block), block)],
            dst_ref=yrecv.at[k - 1],
            send_sem=y_send.at[k - 1],
            recv_sem=y_recv.at[k - 1],
            device_id=(y_peer(k), h),
            device_id_type=MESH,
        )
        for k in range(1, ny)
    ]
    for copy in y_copies:
        copy.start()

    for copy in returns:
        copy.wait_recv()
    gkv_out[...] = (centre[...] + dot(pick_turned[...], returned[...])).astype(BF)
    stores.append(pltpu.make_async_copy(gkv_out.at[:, 0:features], gk_hbm, store_sem.at[1]))
    stores.append(
        pltpu.make_async_copy(gkv_out.at[:, features : 2 * features], gv_hbm, store_sem.at[2])
    )
    stores[1].start()
    stores[2].start()

    for copy in y_copies:
        copy.wait_recv()
    total = ysum[pl.ds(pl.multiple_of(y * block, block), block), :].astype(F32)
    for k in range(ny - 1):
        total = total + yrecv[k].astype(F32)
    zsum[...] = total
    z_copies = [
        pltpu.make_async_remote_copy(
            src_ref=zsum.at[pl.ds(pl.multiple_of(lax.rem(z + k, nz) * rows, rows), rows)],
            dst_ref=zrecv.at[k - 1],
            send_sem=z_send.at[k - 1],
            recv_sem=z_recv.at[k - 1],
            device_id=(z_peer(k), h),
            device_id_type=MESH,
        )
        for k in range(1, nz)
    ]
    for copy in z_copies:
        copy.start()
    for copy in z_copies:
        copy.wait_recv()
    total = zsum[pl.ds(pl.multiple_of(z * rows, rows), rows), :]
    for k in range(nz - 1):
        total = total + zrecv[k]
    gow_out[...] = total * (1.0 / math.sqrt(CELLS * tile_count))
    stores.append(pltpu.make_async_copy(gow_out, gow_hbm, store_sem.at[3]))
    stores[3].start()
    for copy in halos + gathers + x_copies + returns + y_copies + z_copies:
        copy.wait_send()
    for store in stores:
        store.wait()


def shards(queries, keys, values, grad_output, out_weight, rotations):
    tile_count = lax.axis_size("tile")
    tokens, features = queries.shape
    heads = features // HEAD_DIM
    width = out_weight.shape[0]
    rows = width // tile_count
    ny, nz, nx = tile_axes(tile_count)
    anywhere = pl.BlockSpec(memory_space=pl.ANY)
    out = jax.ShapeDtypeStruct((tokens, features), BF)
    dma = pltpu.SemaphoreType.DMA
    return pl.pallas_call(
        functools.partial(kernel, tile_count),
        out_shape=(out, out, out, jax.ShapeDtypeStruct((rows, features), F32)),
        in_specs=[anywhere] * 5 + [pl.BlockSpec(memory_space=pltpu.SMEM)],
        out_specs=(anywhere,) * 4,
        scratch_shapes=[
            pltpu.VMEM((CELLS, features), BF),
            pltpu.VMEM((EXT, 2 * features), BF),
            pltpu.VMEM((4, CELLS, features), BF),
            pltpu.VMEM((4, features, CELLS), BF),
            pltpu.VMEM((width, features), BF),
            pltpu.VMEM((4 * STRIP, CELLS), BF),
            pltpu.VMEM((CELLS, 4 * STRIP), BF),
            pltpu.VMEM((4 * STRIP, 2 * features), BF),
            pltpu.VMEM((EXT, CELLS), F32),
            pltpu.VMEM((heads * CELLS, features), BF),
            pltpu.VMEM((2 * features, EXT), BF),
            pltpu.VMEM((EXT, heads * CELLS), F32),
            pltpu.VMEM((EXT, heads * CELLS), BF),
            pltpu.VMEM((EXT, heads * CELLS), BF),
            pltpu.VMEM((features, CELLS), F32),
            pltpu.VMEM((heads * CELLS, features), BF),
            pltpu.VMEM((heads * features, CELLS), BF),
            pltpu.VMEM((CELLS, 2 * features), F32),
            pltpu.VMEM((4 * STRIP, 2 * features), BF),
            pltpu.VMEM((4 * STRIP, 2 * features), BF),
            pltpu.VMEM((nx, width // nx, features), BF),
            pltpu.VMEM((nx - 1, width // nx, features), BF),
            pltpu.VMEM((width // nx, features), BF),
            pltpu.VMEM((ny - 1, nz * rows, features), BF),
            pltpu.VMEM((nz * rows, features), F32),
            pltpu.VMEM((nz - 1, rows, features), F32),
            pltpu.VMEM((CELLS, features), BF),
            pltpu.VMEM((CELLS, 2 * features), BF),
            pltpu.VMEM((rows, features), F32),
            pltpu.VMEM((features, CELLS), F32),
            dma((5,)),
            dma((4,)),
            dma((3,)),
            dma((3,)),
            dma((4,)),
            dma((4,)),
            dma((4,)),
            dma((4,)),
            dma((nx - 1,)),
            dma((nx - 1,)),
            dma((ny - 1,)),
            dma((ny - 1,)),
            dma((nz - 1,)),
            dma((nz - 1,)),
        ],
        compiler_params=pltpu.CompilerParams(collective_id=0, has_side_effects=True),
    )(queries, keys, values, grad_output, out_weight, rotations)


def solution(mesh):
    placed = (
        P("tile", "head"),
        P("tile", "head"),
        P("tile", "head"),
        P("tile", "head"),
        P(None, "head"),
        P("tile", None),
    )
    return jax.shard_map(
        shards,
        mesh=mesh,
        in_specs=placed,
        out_specs=(P("tile", "head"), P("tile", "head"), P("tile", "head"), P("tile", "head")),
        check_vma=False,
    )
```

time: 911 us -> 51.7 us (0.06)
  the two profiles are of different devices: /device:TPU:32 before, /device:TPU:70 now
where the time goes in v1:
time: 51.7 us; the launch traced here: 51.5 us
  Pallas kernels  47 us (91%)
  local copies, waits for them, and re-layouts  3.85 us (7%)
  between operations  0.65 us (1%)
    pallas_call x1, Pallas kernels, shards(): pl.pallas_call(functools.partial(kernel, tile_count), out_shape=(out, out...  47 us
    unnamed x10, local copies, waits for them, and re-layouts  3.85 us

profile of v1, /device:TPU:70, one launch (start us, length us, event | category | flops | bytes accessed | tf_op | source)
XLA Modules:
  0.0 51.5 jit_solution(2575780375028245074)
XLA Ops:
  0.6 47.0 %shard_map.93 = (bf16[256,256]{1,0:T(8,128)(2,1)}, bf16[256,256]{1,0:T(8,128)(2,1)}, bf16[256,256]{1,0:T(8,128)(2,1)}, f32[8,256]{1,0:T(8,128)}) custom-call(bf16[256,256]{1,0:T(8,128)(2,1)} %q_hbm.1, bf16[256,256]{1,0:T(8,128)(2,1)} %k_hbm.1, bf16[256,256]{1,0:T(8,128)(2,1)} %v_hbm.1, bf16[256,256]{1,0:T(8,128)(2,1)} %g_hbm.1, bf16[1024,256]{1,0:T(8,128)(2,1)} %w_hbm.1, ...), custom_call_target="tpu_custom_call" | custom-call | tf_op jit(solution)/shard_map/pallas_call | solution.py:415
  47.6 0.0 copy-start.1
  47.7 1.6 %copy.14 = bf16[256,256]{1,0:T(8,128)(2,1)} copy(bf16[256,256]{1,0:T(8,128)(2,1)} %get-tuple-element.8) | data formatting | bytes 262144
  49.3 0.0 copy-done.1
  49.3 0.0 copy-start
  49.3 0.7 %copy.15 = bf16[256,256]{1,0:T(8,128)(2,1)} copy(bf16[256,256]{1,0:T(8,128)(2,1)S(1)} %copy-done.1) | data formatting | bytes 262144
  49.9 0.3 copy-done
  50.2 0.0 copy-start.2
  50.2 0.7 %copy.16 = bf16[256,256]{1,0:T(8,128)(2,1)} copy(bf16[256,256]{1,0:T(8,128)(2,1)S(1)} %copy-done) | data formatting | bytes 262144
  50.9 0.0 copy-done.2
  50.9 0.6 %copy.17 = f32[8,256]{1,0:T(8,128)} copy(f32[8,256]{1,0:T(8,128)S(1)} %copy-done.2) | data formatting | bytes 16384
Async XLA Ops:
  47.6 1.6 %copy-start.1 = (bf16[256,256]{1,0:T(8,128)(2,1)S(1)}, bf16[256,256]{1,0:T(8,128)(2,1)}, u32[]{:S(2)}) copy-start(bf16[256,256]{1,0:T(8,128)(2,1)} %get-tuple-element.9) | copy-start | bytes 393220
  49.3 1.0 %copy-start = (bf16[256,256]{1,0:T(8,128)(2,1)S(1)}, bf16[256,256]{1,0:T(8,128)(2,1)}, u32[]{:S(2)}) copy-start(bf16[256,256]{1,0:T(8,128)(2,1)} %get-tuple-element.10) | copy-start | bytes 393220
  50.2 0.7 %copy-start.2 = (f32[8,256]{1,0:T(8,128)S(1)}, f32[8,256]{1,0:T(8,128)}, u32[]{:S(2)}) copy-start(f32[8,256]{1,0:T(8,128)} %get-tuple-element.11) | copy-start | bytes 24580

commit v2 on v1

v2 whole, which is shorter than its diff:
```python
import functools
import math

import jax
import jax.numpy as jnp
from jax import lax
from jax.experimental import pallas as pl
from jax.experimental.pallas import tpu as pltpu
from jax.sharding import PartitionSpec as P

HEAD_DIM = 64
RADIUS = 6
SIDE = 16
CELLS = SIDE * SIDE
STRIP = RADIUS * SIDE
EXT = CELLS + 4 * STRIP
MESH = pl.DeviceIdType.MESH
BF = jnp.bfloat16
F32 = jnp.float32
NT = (((1,), (1,)), ((), ()))


def dot(a, b):
    return jnp.dot(a, b, preferred_element_type=F32)


def dot_nt(a, b):
    return lax.dot_general(a, b, NT, preferred_element_type=F32)


def tile_axes(tile_count):
    return {128: (8, 4, 4), 8: (2, 2, 2)}[tile_count]


def kernel(
    tile_count,
    q_hbm,
    k_hbm,
    v_hbm,
    g_hbm,
    w_hbm,
    rot_ref,
    gq_hbm,
    gk_hbm,
    gv_hbm,
    gow_hbm,
    qbuf,
    kbuf,
    vbuf,
    gbuf,
    gturned,
    wbuf,
    pick,
    pick_turned,
    kstrips,
    vstrips,
    bias,
    qstack,
    kt,
    vt,
    weights,
    weights_bf,
    dscore,
    att_t,
    dstack,
    dturned,
    centre_k,
    centre_v,
    kback,
    vback,
    kreturned,
    vreturned,
    xsend,
    xrecv,
    ysum,
    yrecv,
    zsum,
    zrecv,
    gq_out,
    gk_out,
    gv_out,
    gow_out,
    gq_t,
    load_sem,
    store_sem,
    ag_send,
    ag_recv,
    halo_send,
    halo_recv,
    ret_send,
    ret_recv,
    x_send,
    x_recv,
    y_send,
    y_recv,
    z_send,
    z_recv,
):
    ny, nz, nx = tile_axes(tile_count)
    features = q_hbm.shape[1]
    heads = features // HEAD_DIM
    rows = gow_hbm.shape[0]
    t = lax.axis_index("tile")
    h = lax.axis_index("head")
    x = lax.rem(t, nx)
    z = lax.rem(t // nx, nz)
    y = t // (nx * nz)
    h1 = h + 1 - 2 * lax.rem(h, 2)
    h2 = lax.rem(h + 2, 4)
    h3 = 3 - h

    def at_xyz(yy, zz, xx):
        return (yy * nz + zz) * nx + xx

    def x_peer(k):
        return at_xyz(y, z, lax.rem(x + k, nx))

    def y_peer(k):
        return at_xyz(lax.rem(y + k, ny), z, x)

    def z_peer(k):
        return at_xyz(y, lax.rem(z + k, nz), x)

    offsets = (-(tile_count // 4), 1, tile_count // 4, -1)

    def beside(side):
        return lax.rem(t + offsets[side] + tile_count, tile_count)

    loads = [
        pltpu.make_async_copy(k_hbm, kbuf.at[0:CELLS], load_sem.at[0]),
        pltpu.make_async_copy(v_hbm, vbuf.at[0:CELLS], load_sem.at[1]),
        pltpu.make_async_copy(q_hbm, qbuf, load_sem.at[2]),
        pltpu.make_async_copy(g_hbm, gbuf.at[0], load_sem.at[3]),
        pltpu.make_async_copy(w_hbm, wbuf, load_sem.at[4]),
    ]
    barrier = pltpu.get_barrier_semaphore()
    peers = [(t, h1), (t, h2), (t, h3)]
    peers += [(beside(side), h) for side in range(4)]
    peers += [(y_peer(k), h) for k in range(1, ny)]
    peers += [(x_peer(k), h) for k in range(1, nx)]
    peers += [(z_peer(k), h) for k in range(1, nz)]
    for peer in peers:
        pl.semaphore_signal(barrier, inc=1, device_id=peer, device_id_type=MESH)
    for load in loads:
        load.start()

    starts, down, along = [], [], []
    for side in range(4):
        turn = lax.rem(side + 4 - rot_ref[0, (side + 2) % 4], 4)

        def choose(a, b, c, d, turn=turn):
            return jnp.where(turn == 0, a, jnp.where(turn == 1, b, jnp.where(turn == 2, c, d)))

        starts.append(choose(160, 5, 95, 250))
        down.append(choose(16, -1, -16, 1))
        along.append(choose(1, 16, -1, -16))
    place = lax.broadcasted_iota(jnp.int32, (STRIP, CELLS), 0)
    cell = lax.broadcasted_iota(jnp.int32, (STRIP, CELLS), 1)
    for side in range(4):
        target = starts[side] + down[side] * (place // SIDE) + along[side] * (place % SIDE)
        pick[side * STRIP : (side + 1) * STRIP, :] = jnp.where(cell == target, 1.0, 0.0).astype(BF)
    loads[0].wait()
    kstrips[...] = dot(pick[...], kbuf[0:CELLS, :]).astype(BF)
    loads[1].wait()
    vstrips[...] = dot(pick[...], vbuf[0:CELLS, :]).astype(BF)

    def halo(number, source, target, side):
        return pltpu.make_async_remote_copy(
            src_ref=source.at[side * STRIP : (side + 1) * STRIP],
            dst_ref=target.at[CELLS + side * STRIP : CELLS + (side + 1) * STRIP],
            send_sem=halo_send.at[number, side],
            recv_sem=halo_recv.at[number, side],
            device_id=(beside((side + 2) % 4), h),
            device_id_type=MESH,
        )

    order = (1, 3, 0, 2)
    key_halos = [halo(0, kstrips, kbuf, side) for side in order]
    value_halos = [halo(1, vstrips, vbuf, side) for side in order]
    gathers = [
        pltpu.make_async_remote_copy(
            src_ref=source,
            dst_ref=gbuf.at[slot],
            send_sem=ag_send.at[slot - 1],
            recv_sem=ag_recv.at[slot - 1],
            device_id=(t, peer),
            device_id_type=MESH,
        )
        for slot, source, peer in ((1, g_hbm, h1), (2, g_hbm, h2), (3, gbuf.at[2], h1))
    ]
    pl.semaphore_wait(barrier, len(peers))
    for copy in key_halos:
        copy.start()
    gathers[1].start()
    gathers[0].start()
    for copy in value_halos:
        copy.start()

    cell_t = lax.broadcasted_iota(jnp.int32, (CELLS, 4 * STRIP), 0)
    place_t = lax.broadcasted_iota(jnp.int32, (CELLS, 4 * STRIP), 1)
    side_t = place_t // STRIP
    rest_t = place_t - side_t * STRIP

    def by_side(values):
        return jnp.where(
            side_t == 0,
            values[0],
            jnp.where(side_t == 1, values[1], jnp.where(side_t == 2, values[2], values[3])),
        )

    target_t = by_side(starts) + by_side(down) * (rest_t // SIDE) + by_side(along) * (rest_t % SIDE)
    pick_turned[...] = jnp.where(cell_t == target_t, 1.0, 0.0).astype(BF)

    def fill_bias(first, count, where_is):
        index = lax.broadcasted_iota(jnp.int32, (count, CELLS), 0)
        query = lax.broadcasted_iota(jnp.int32, (count, CELLS), 1)
        a, b = where_is(index // SIDE, index % SIDE)
        off_a = a - query // SIDE
        off_b = b - query % SIDE
        inside = (off_a >= 0) & (off_a <= 2 * RADIUS) & (off_b >= 0) & (off_b <= 2 * RADIUS)
        bias[first : first + count, :] = jnp.where(inside, 0.0, -1e30)

    last = SIDE + 2 * RADIUS - 1
    fill_bias(0, CELLS, lambda i, j: (i + RADIUS, j + RADIUS))
    fill_bias(CELLS, STRIP, lambda i, j: (i, RADIUS + j))
    fill_bias(CELLS + STRIP, STRIP, lambda i, j: (RADIUS + j, last - i))
    fill_bias(CELLS + 2 * STRIP, STRIP, lambda i, j: (last - i, last - RADIUS - j))
    fill_bias(CELLS + 3 * STRIP, STRIP, lambda i, j: (last - RADIUS - j, i))

    loads[2].wait()
    lane = lax.broadcasted_iota(jnp.int32, (CELLS, features), 1)
    scaled = qbuf[...].astype(F32) * (HEAD_DIM ** (-0.5))
    for head in range(heads):
        own = lane // HEAD_DIM == head
        qstack[head * CELLS : (head + 1) * CELLS, :] = jnp.where(own, scaled, 0.0).astype(BF)

    pieces = 3
    piece = 4 * STRIP // pieces
    own_tops = []
    for head in range(heads):
        cols = slice(head * CELLS, (head + 1) * CELLS)
        score = dot_nt(kbuf[0:CELLS, :], qstack[cols, :])
        top = None
        for n in range(2):
            part = slice(n * 128, (n + 1) * 128)
            masked = score[part] + bias[part, :]
            weights[part, cols] = masked
            highest = jnp.max(masked.reshape(16, 8, CELLS), axis=0)
            top = highest if top is None else jnp.maximum(top, highest)
        own_tops.append(top)
    vt[:, 0:CELLS] = vbuf[0:CELLS, :].T
    loads[3].wait()
    gturned[0] = gbuf[0].T
    gathers[1].wait_recv()
    gathers[2].start()
    gturned[2] = gbuf[2].T
    gathers[0].wait_recv()
    gturned[1] = gbuf[1].T

    for copy in key_halos:
        copy.wait_recv()
    for head in range(heads):
        cols = slice(head * CELLS, (head + 1) * CELLS)
        score = dot_nt(kbuf[CELLS:EXT, :], qstack[cols, :])
        top = own_tops[head]
        for n in range(pieces):
            part = slice(CELLS + n * piece, CELLS + (n + 1) * piece)
            masked = score[n * piece : (n + 1) * piece] + bias[part, :]
            weights[part, cols] = masked
            top = jnp.maximum(top, jnp.max(masked.reshape(piece // 8, 8, CELLS), axis=0))
        top = jnp.max(top, axis=0, keepdims=True)
        total = None
        for n in range(5):
            part = slice(n * 128, (n + 1) * 128)
            raw = jnp.exp(weights[part, cols] - top)
            weights[part, cols] = raw
            summed = jnp.sum(raw.reshape(16, 8, CELLS), axis=0)
            total = summed if total is None else total + summed
        inverse = 1.0 / jnp.sum(total, axis=0, keepdims=True)
        for n in range(5):
            part = slice(n * 128, (n + 1) * 128)
            normal = weights[part, cols] * inverse
            weights[part, cols] = normal
            weights_bf[part, cols] = normal.astype(BF)
    gathers[2].wait_recv()
    gturned[3] = gbuf[3].T
    for copy in value_halos:
        copy.wait_recv()
    vt[:, CELLS:EXT] = vbuf[CELLS:EXT, :].T

    holders = (h, h1, h2, h3)
    half = features // 2
    per_slot = features // rows // nx * rows
    x_copies, y_copies = [], []
    for part in range(2):
        for head in range(part * heads // 2, (part + 1) * heads // 2):
            own_rows = slice(head * HEAD_DIM, (head + 1) * HEAD_DIM)
            att_t[own_rows, :] = dot(
                vt[own_rows, :], weights_bf[:, head * CELLS : (head + 1) * CELLS]
            )
        att_bf = att_t[part * half : (part + 1) * half, :].astype(BF)
        for slot in range(4):
            term = dot_nt(gturned[slot], att_bf)
            term = term.reshape(per_slot // rows, nx, rows, half)
            first = pl.multiple_of(holders[slot] * per_slot, per_slot)
            for xx in range(nx):
                xsend[part, xx, pl.ds(first, per_slot), :] = (
                    term[:, xx].reshape(per_slot, half).astype(BF)
                )
        x_copies.append(
            [
                pltpu.make_async_remote_copy(
                    src_ref=xsend.at[part, lax.rem(x + k, nx)],
                    dst_ref=xrecv.at[part, k - 1],
                    send_sem=x_send.at[part, k - 1],
                    recv_sem=x_recv.at[part, k - 1],
                    device_id=(x_peer(k), h),
                    device_id_type=MESH,
                )
                for k in range(1, nx)
            ]
        )
        for copy in x_copies[part]:
            copy.start()

    loads[4].wait()
    dout = None
    for slot in range(4):
        first = pl.multiple_of(holders[slot] * features, features)
        term = dot(gbuf[slot], wbuf[pl.ds(first, features), :])
        dout = term if dout is None else dout + term
    dout = dout.astype(BF).astype(F32)
    for head in range(heads):
        own = lane // HEAD_DIM == head
        dstack[head * CELLS : (head + 1) * CELLS, :] = jnp.where(own, dout, 0.0).astype(BF)

    def give_back(number, source, target, side):
        return pltpu.make_async_remote_copy(
            src_ref=source.at[side * STRIP : (side + 1) * STRIP],
            dst_ref=target.at[side * STRIP : (side + 1) * STRIP],
            send_sem=ret_send.at[number, side],
            recv_sem=ret_recv.at[number, side],
            device_id=(beside(side), h),
            device_id_type=MESH,
        )

    vback[...] = dot(weights_bf[CELLS:EXT, :], dstack[...]).astype(BF)
    value_returns = [give_back(1, vback, vreturned, side) for side in order]
    for copy in value_returns:
        copy.start()
    dout_t = dout.T
    row = lax.broadcasted_iota(jnp.int32, (features, CELLS), 0)
    product = dout_t * att_t[...]
    for head in range(heads):
        own = row // HEAD_DIM == head
        dturned[head * features : (head + 1) * features, :] = jnp.where(own, dout_t, 0.0).astype(BF)
    for head in range(heads):
        cols = slice(head * CELLS, (head + 1) * CELLS)
        own_rows = slice(head * HEAD_DIM, (head + 1) * HEAD_DIM)
        delta = jnp.sum(product[own_rows], axis=0, keepdims=True)
        grad_weight = dot(vbuf[...], dturned[head * features : (head + 1) * features, :])
        for n in range(5):
            part = slice(n * 128, (n + 1) * 128)
            dscore[part, cols] = (weights[part, cols] * (grad_weight[part] - delta)).astype(BF)
    kback[...] = dot(dscore[CELLS:EXT, :], qstack[...]).astype(BF)
    key_returns = [give_back(0, kback, kreturned, side) for side in order]
    for copy in key_returns:
        copy.start()

    block = nz * rows

    def sum_over_x(part):
        for copy in x_copies[part]:
            copy.wait_recv()
        total = xsend[part, x].astype(F32)
        for k in range(nx - 1):
            total = total + xrecv[part, k].astype(F32)
        ysum[part] = total.astype(BF)
        y_copies.append(
            [
                pltpu.make_async_remote_copy(
                    src_ref=ysum.at[
                        part, pl.ds(pl.multiple_of(lax.rem(y + k, ny) * block, block), block)
                    ],
                    dst_ref=yrecv.at[part, k - 1],
                    send_sem=y_send.at[part, k - 1],
                    recv_sem=y_recv.at[part, k - 1],
                    device_id=(y_peer(k), h),
                    device_id_type=MESH,
                )
                for k in range(1, ny)
            ]
        )
        for copy in y_copies[part]:
            copy.start()

    sum_over_x(0)
    centre_v[...] = dot(weights_bf[0:CELLS, :], dstack[...])
    sum_over_x(1)
    centre_k[...] = dot(dscore[0:CELLS, :], qstack[...])
    kt[...] = kbuf[...].T
    for head in range(heads):
        own_rows = slice(head * HEAD_DIM, (head + 1) * HEAD_DIM)
        gq_t[own_rows, :] = dot(kt[own_rows, :], dscore[:, head * CELLS : (head + 1) * CELLS])
    gq_out[...] = (gq_t[...].T * (HEAD_DIM ** (-0.5))).astype(BF)
    stores = [pltpu.make_async_copy(gq_out, gq_hbm, store_sem.at[0])]
    stores[0].start()

    for part in range(2):
        for copy in y_copies[part]:
            copy.wait_recv()
        total = ysum[part, pl.ds(pl.multiple_of(y * block, block), block), :].astype(F32)
        for k in range(ny - 1):
            total = total + yrecv[part, k].astype(F32)
        zsum[:, part * half : (part + 1) * half] = total
    z_copies = [
        pltpu.make_async_remote_copy(
            src_ref=zsum.at[pl.ds(pl.multiple_of(lax.rem(z + k, nz) * rows, rows), rows)],
            dst_ref=zrecv.at[k - 1],
            send_sem=z_send.at[k - 1],
            recv_sem=z_recv.at[k - 1],
            device_id=(z_peer(k), h),
            device_id_type=MESH,
        )
        for k in range(1, nz)
    ]
    for copy in z_copies:
        copy.start()

    for copy in value_returns:
        copy.wait_recv()
    gv_out[...] = (centre_v[...] + dot(pick_turned[...], vreturned[...])).astype(BF)
    stores.append(pltpu.make_async_copy(gv_out, gv_hbm, store_sem.at[2]))
    stores[1].start()
    for copy in key_returns:
        copy.wait_recv()
    gk_out[...] = (centre_k[...] + dot(pick_turned[...], kreturned[...])).astype(BF)
    stores.append(pltpu.make_async_copy(gk_out, gk_hbm, store_sem.at[1]))
    stores[2].start()

    for copy in z_copies:
        copy.wait_recv()
    total = zsum[pl.ds(pl.multiple_of(z * rows, rows), rows), :]
    for k in range(nz - 1):
        total = total + zrecv[k]
    gow_out[...] = total * (1.0 / math.sqrt(CELLS * tile_count))
    stores.append(pltpu.make_async_copy(gow_out, gow_hbm, store_sem.at[3]))
    stores[3].start()
    sent = key_halos + value_halos + gathers + key_returns + value_returns + z_copies
    for copy in sent + x_copies[0] + x_copies[1] + y_copies[0] + y_copies[1]:
        copy.wait_send()
    for store in stores:
        store.wait()


def handed_on(*refs):
    sources, targets, sems = refs[:4], refs[4:8], refs[8]
    copies = [pltpu.make_async_copy(a, b, sems.at[n]) for n, (a, b) in enumerate(zip(sources, targets))]
    for copy in copies:
        copy.start()
    for copy in copies:
        copy.wait()


def shards(queries, keys, values, grad_output, out_weight, rotations):
    tile_count = lax.axis_size("tile")
    tokens, features = queries.shape
    heads = features // HEAD_DIM
    width = out_weight.shape[0]
    rows = width // tile_count
    ny, nz, nx = tile_axes(tile_count)
    anywhere = pl.BlockSpec(memory_space=pl.ANY)
    out = jax.ShapeDtypeStruct((tokens, features), BF)
    dma = pltpu.SemaphoreType.DMA
    results = pl.pallas_call(
        functools.partial(kernel, tile_count),
        out_shape=(out, out, out, jax.ShapeDtypeStruct((rows, features), F32)),
        in_specs=[anywhere] * 5 + [pl.BlockSpec(memory_space=pltpu.SMEM)],
        out_specs=(pl.BlockSpec(memory_space=pltpu.VMEM),) * 4,
        scratch_shapes=[
            pltpu.VMEM((CELLS, features), BF),
            pltpu.VMEM((EXT, features), BF),
            pltpu.VMEM((EXT, features), BF),
            pltpu.VMEM((4, CELLS, features), BF),
            pltpu.VMEM((4, features, CELLS), BF),
            pltpu.VMEM((width, features), BF),
            pltpu.VMEM((4 * STRIP, CELLS), BF),
            pltpu.VMEM((CELLS, 4 * STRIP), BF),
            pltpu.VMEM((4 * STRIP, features), BF),
            pltpu.VMEM((4 * STRIP, features), BF),
            pltpu.VMEM((EXT, CELLS), F32),
            pltpu.VMEM((heads * CELLS, features), BF),
            pltpu.VMEM((features, EXT), BF),
            pltpu.VMEM((features, EXT), BF),
            pltpu.VMEM((EXT, heads * CELLS), F32),
            pltpu.VMEM((EXT, heads * CELLS), BF),
            pltpu.VMEM((EXT, heads * CELLS), BF),
            pltpu.VMEM((features, CELLS), F32),
            pltpu.VMEM((heads * CELLS, features), BF),
            pltpu.VMEM((heads * features, CELLS), BF),
            pltpu.VMEM((CELLS, features), F32),
            pltpu.VMEM((CELLS, features), F32),
            pltpu.VMEM((4 * STRIP, features), BF),
            pltpu.VMEM((4 * STRIP, features), BF),
            pltpu.VMEM((4 * STRIP, features), BF),
            pltpu.VMEM((4 * STRIP, features), BF),
            pltpu.VMEM((2, nx, width // nx, features // 2), BF),
            pltpu.VMEM((2, nx - 1, width // nx, features // 2), BF),
            pltpu.VMEM((2, width // nx, features // 2), BF),
            pltpu.VMEM((2, ny - 1, nz * rows, features // 2), BF),
            pltpu.VMEM((nz * rows, features), F32),
            pltpu.VMEM((nz - 1, rows, features), F32),
            pltpu.VMEM((CELLS, features), BF),
            pltpu.VMEM((CELLS, features), BF),
            pltpu.VMEM((CELLS, features), BF),
            pltpu.VMEM((rows, features), F32),
            pltpu.VMEM((features, CELLS), F32),
            dma((5,)),
            dma((4,)),
            dma((3,)),
            dma((3,)),
            dma((2, 4)),
            dma((2, 4)),
            dma((2, 4)),
            dma((2, 4)),
            dma((2, nx - 1)),
            dma((2, nx - 1)),
            dma((2, ny - 1)),
            dma((2, ny - 1)),
            dma((nz - 1,)),
            dma((nz - 1,)),
        ],
        compiler_params=pltpu.CompilerParams(collective_id=0, has_side_effects=True),
    )(queries, keys, values, grad_output, out_weight, rotations)
    return pl.pallas_call(
        handed_on,
        out_shape=(out, out, out, jax.ShapeDtypeStruct((rows, features), F32)),
        in_specs=[pl.BlockSpec(memory_space=pltpu.VMEM)] * 4,
        out_specs=(anywhere,) * 4,
        scratch_shapes=[dma((4,))],
    )(*results)


def solution(mesh):
    placed = (
        P("tile", "head"),
        P("tile", "head"),
        P("tile", "head"),
        P("tile", "head"),
        P(None, "head"),
        P("tile", None),
    )
    return jax.shard_map(
        shards,
        mesh=mesh,
        in_specs=placed,
        out_specs=(P("tile", "head"), P("tile", "head"), P("tile", "head"), P("tile", "head")),
        check_vma=False,
    )
```

time: 51.7 us -> 48.2 us (0.932)
  the two profiles are of different devices: /device:TPU:70 before, /device:TPU:4 now
where the time goes in v2:
time: 48.2 us; the launch traced here: 48 us
  Pallas kernels  47.4 us (98%)
  between operations  0.64 us (1%)
    pallas_call x1, Pallas kernels, shards(): pl.pallas_call(functools.partial(kernel, tile_count), out_shape=(out, out...  45.6 us
    pallas_call x1, Pallas kernels, shards(): pl.pallas_call(handed_on, out_shape=(out, out, out, jax.ShapeDtypeStruct(...  1.81 us

profile of v2, /device:TPU:4, one launch (start us, length us, event | category | flops | bytes accessed | tf_op | source)
XLA Modules:
  0.0 48.0 jit_solution(6433956643434529597)
XLA Ops:
  0.6 45.6 %shard_map.93 = (bf16[256,256]{1,0:T(8,128)(2,1)}, bf16[256,256]{1,0:T(8,128)(2,1)}, bf16[256,256]{1,0:T(8,128)(2,1)}, f32[8,256]{1,0:T(8,128)}) custom-call(bf16[256,256]{1,0:T(8,128)(2,1)} %q_hbm.1, bf16[256,256]{1,0:T(8,128)(2,1)} %k_hbm.1, bf16[256,256]{1,0:T(8,128)(2,1)} %v_hbm.1, bf16[256,256]{1,0:T(8,128)(2,1)} %g_hbm.1, bf16[1024,256]{1,0:T(8,128)(2,1)} %w_hbm.1, ...), custom_call_target="tpu_custom_call" | custom-call | tf_op jit(solution)/shard_map/pallas_call | solution.py:475
  46.2 1.8 %shard_map.94 = (bf16[256,256]{1,0:T(8,128)(2,1)}, bf16[256,256]{1,0:T(8,128)(2,1)}, bf16[256,256]{1,0:T(8,128)(2,1)}, f32[8,256]{1,0:T(8,128)}) custom-call(bf16[256,256]{1,0:T(8,128)(2,1)} %get-tuple-element.8.refs_0_, bf16[256,256]{1,0:T(8,128)(2,1)} %get-tuple-element.9.refs_1_, bf16[256,256]{1,0:T(8,128)(2,1)} %get-tuple-element.10.refs_2_, ...), custom_call_target="tpu_custom_call" | custom-call | tf_op jit(solution)/shard_map/pallas_call | solution.py:535

commit v3 on v2

--- a/solution.py
+++ b/solution.py
@@ -128,10 +128,18 @@
 
     loads = [
         pltpu.make_async_copy(k_hbm, kbuf.at[0:CELLS], load_sem.at[0]),
-        pltpu.make_async_copy(v_hbm, vbuf.at[0:CELLS], load_sem.at[1]),
         pltpu.make_async_copy(q_hbm, qbuf, load_sem.at[2]),
         pltpu.make_async_copy(g_hbm, gbuf.at[0], load_sem.at[3]),
         pltpu.make_async_copy(w_hbm, wbuf, load_sem.at[4]),
+    ]
+    half = features // 2
+    value_loads = [
+        pltpu.make_async_copy(
+            v_hbm.at[:, part * half : (part + 1) * half],
+            vbuf.at[part, 0:CELLS],
+            load_sem.at[(1, 5)[part]],
+        )
+        for part in range(2)
     ]
     barrier = pltpu.get_barrier_semaphore()
     peers = [(t, h1), (t, h2), (t, h3)]
@@ -141,7 +149,7 @@
     peers += [(z_peer(k), h) for k in range(1, nz)]
     for peer in peers:
         pl.semaphore_signal(barrier, inc=1, device_id=peer, device_id_type=MESH)
-    for load in loads:
+    for load in loads[:1] + value_loads + loads[1:]:
         load.start()
 
     starts, down, along = [], [], []
@@ -161,8 +169,9 @@
         pick[side * STRIP : (side + 1) * STRIP, :] = jnp.where(cell == target, 1.0, 0.0).astype(BF)
     loads[0].wait()
     kstrips[...] = dot(pick[...], kbuf[0:CELLS, :]).astype(BF)
-    loads[1].wait()
-    vstrips[...] = dot(pick[...], vbuf[0:CELLS, :]).astype(BF)
+    for part in range(2):
+        value_loads[part].wait()
+        vstrips[part] = dot(pick[...], vbuf[part, 0:CELLS, :]).astype(BF)
 
     def halo(number, source, target, side):
         return pltpu.make_async_remote_copy(
@@ -176,7 +185,10 @@
 
     order = (1, 3, 0, 2)
     key_halos = [halo(0, kstrips, kbuf, side) for side in order]
-    value_halos = [halo(1, vstrips, vbuf, side) for side in order]
+    value_halos = [
+        [halo(1 + part, vstrips.at[part], vbuf.at[part], side) for side in order]
+        for part in range(2)
+    ]
     gathers = [
         pltpu.make_async_remote_copy(
             src_ref=source,
@@ -191,9 +203,11 @@
     pl.semaphore_wait(barrier, len(peers))
     for copy in key_halos:
         copy.start()
+    gathers[0].start()
+    for copy in value_halos[0]:
+        copy.start()
     gathers[1].start()
-    gathers[0].start()
-    for copy in value_halos:
+    for copy in value_halos[1]:
         copy.start()
 
     cell_t = lax.broadcasted_iota(jnp.int32, (CELLS, 4 * STRIP), 0)
@@ -227,7 +241,7 @@
     fill_bias(CELLS + 2 * STRIP, STRIP, lambda i, j: (last - i, last - RADIUS - j))
     fill_bias(CELLS + 3 * STRIP, STRIP, lambda i, j: (last - RADIUS - j, i))
 
-    loads[2].wait()
+    loads[1].wait()
     lane = lax.broadcasted_iota(jnp.int32, (CELLS, features), 1)
     scaled = qbuf[...].astype(F32) * (HEAD_DIM ** (-0.5))
     for head in range(heads):
@@ -248,8 +262,9 @@
             highest = jnp.max(masked.reshape(16, 8, CELLS), axis=0)
             top = highest if top is None else jnp.maximum(top, highest)
         own_tops.append(top)
-    vt[:, 0:CELLS] = vbuf[0:CELLS, :].T
-    loads[3].wait()
+    for part in range(2):
+        vt[part * half : (part + 1) * half, 0:CELLS] = vbuf[part, 0:CELLS, :].T
+    loads[2].wait()
     gturned[0] = gbuf[0].T
     gathers[1].wait_recv()
     gathers[2].start()
@@ -284,15 +299,14 @@
             weights_bf[part, cols] = normal.astype(BF)
     gathers[2].wait_recv()
     gturned[3] = gbuf[3].T
-    for copy in value_halos:
-        copy.wait_recv()
-    vt[:, CELLS:EXT] = vbuf[CELLS:EXT, :].T
 
     holders = (h, h1, h2, h3)
-    half = features // 2
     per_slot = features // rows // nx * rows
     x_copies, y_copies = [], []
     for part in range(2):
+        for copy in value_halos[part]:
+            copy.wait_recv()
+        vt[part * half : (part + 1) * half, CELLS:EXT] = vbuf[part, CELLS:EXT, :].T
         for head in range(part * heads // 2, (part + 1) * heads // 2):
             own_rows = slice(head * HEAD_DIM, (head + 1) * HEAD_DIM)
             att_t[own_rows, :] = dot(
@@ -323,7 +337,7 @@
         for copy in x_copies[part]:
             copy.start()
 
-    loads[4].wait()
+    loads[3].wait()
     dout = None
     for slot in range(4):
         first = pl.multiple_of(holders[slot] * features, features)
@@ -349,16 +363,19 @@
     for copy in value_returns:
         copy.start()
     dout_t = dout.T
-    row = lax.broadcasted_iota(jnp.int32, (features, CELLS), 0)
+    row = lax.broadcasted_iota(jnp.int32, (half, CELLS), 0)
     product = dout_t * att_t[...]
     for head in range(heads):
-        own = row // HEAD_DIM == head
-        dturned[head * features : (head + 1) * features, :] = jnp.where(own, dout_t, 0.0).astype(BF)
+        part = 2 * head // heads
+        own = row // HEAD_DIM + part * half // HEAD_DIM == head
+        dturned[head * half : (head + 1) * half, :] = jnp.where(
+            own, dout_t[part * half : (part + 1) * half], 0.0
+        ).astype(BF)
     for head in range(heads):
         cols = slice(head * CELLS, (head + 1) * CELLS)
         own_rows = slice(head * HEAD_DIM, (head + 1) * HEAD_DIM)
         delta = jnp.sum(product[own_rows], axis=0, keepdims=True)
-        grad_weight = dot(vbuf[...], dturned[head * features : (head + 1) * features, :])
+        grad_weight = dot(vbuf[2 * head // heads], dturned[head * half : (head + 1) * half, :])
         for n in range(5):
             part = slice(n * 128, (n + 1) * 128)
             dscore[part, cols] = (weights[part, cols] * (grad_weight[part] - delta)).astype(BF)
@@ -446,7 +463,7 @@
     gow_out[...] = total * (1.0 / math.sqrt(CELLS * tile_count))
     stores.append(pltpu.make_async_copy(gow_out, gow_hbm, store_sem.at[3]))
     stores[3].start()
-    sent = key_halos + value_halos + gathers + key_returns + value_returns + z_copies
+    sent = key_halos + value_halos[0] + value_halos[1] + gathers + key_returns + value_returns + z_copies
     for copy in sent + x_copies[0] + x_copies[1] + y_copies[0] + y_copies[1]:
         copy.wait_send()
     for store in stores:
@@ -454,11 +471,15 @@
 
 
 def handed_on(*refs):
-    sources, targets, sems = refs[:4], refs[4:8], refs[8]
-    copies = [pltpu.make_async_copy(a, b, sems.at[n]) for n, (a, b) in enumerate(zip(sources, targets))]
-    for copy in copies:
-        copy.start()
-    for copy in copies:
+    sources, targets, held, sems = refs[:4], refs[4:8], refs[8:12], refs[12]
+    taken = [pltpu.make_async_copy(sources[n], held[n], sems.at[0, n]) for n in range(4)]
+    given = [pltpu.make_async_copy(held[n], targets[n], sems.at[1, n]) for n in range(4)]
+    for copy in taken:
+        copy.start()
+    for n in range(4):
+        taken[n].wait()
+        given[n].start()
+    for copy in given:
         copy.wait()
 
 
@@ -480,14 +501,14 @@
         scratch_shapes=[
             pltpu.VMEM((CELLS, features), BF),
             pltpu.VMEM((EXT, features), BF),
-            pltpu.VMEM((EXT, features), BF),
+            pltpu.VMEM((2, EXT, features // 2), BF),
             pltpu.VMEM((4, CELLS, features), BF),
             pltpu.VMEM((4, features, CELLS), BF),
             pltpu.VMEM((width, features), BF),
             pltpu.VMEM((4 * STRIP, CELLS), BF),
             pltpu.VMEM((CELLS, 4 * STRIP), BF),
             pltpu.VMEM((4 * STRIP, features), BF),
-            pltpu.VMEM((4 * STRIP, features), BF),
+            pltpu.VMEM((2, 4 * STRIP, features // 2), BF),
             pltpu.VMEM((EXT, CELLS), F32),
             pltpu.VMEM((heads * CELLS, features), BF),
             pltpu.VMEM((features, EXT), BF),
@@ -497,7 +518,7 @@
             pltpu.VMEM((EXT, heads * CELLS), BF),
             pltpu.VMEM((features, CELLS), F32),
             pltpu.VMEM((heads * CELLS, features), BF),
-            pltpu.VMEM((heads * features, CELLS), BF),
+            pltpu.VMEM((heads * features // 2, CELLS), BF),
             pltpu.VMEM((CELLS, features), F32),
             pltpu.VMEM((CELLS, features), F32),
             pltpu.VMEM((4 * STRIP, features), BF),
@@ -515,12 +536,12 @@
             pltpu.VMEM((CELLS, features), BF),
             pltpu.VMEM((rows, features), F32),
             pltpu.VMEM((features, CELLS), F32),
-            dma((5,)),
+            dma((6,)),
             dma((4,)),
             dma((3,)),
             dma((3,)),
-            dma((2, 4)),
-            dma((2, 4)),
+            dma((3, 4)),
+            dma((3, 4)),
             dma((2, 4)),
             dma((2, 4)),
             dma((2, nx - 1)),
@@ -535,9 +556,10 @@
     return pl.pallas_call(
         handed_on,
         out_shape=(out, out, out, jax.ShapeDtypeStruct((rows, features), F32)),
-        in_specs=[pl.BlockSpec(memory_space=pltpu.VMEM)] * 4,
+        in_specs=[anywhere] * 4,
         out_specs=(anywhere,) * 4,
-        scratch_shapes=[dma((4,))],
+        scratch_shapes=[pltpu.VMEM((tokens, features), BF)] * 3
+        + [pltpu.VMEM((rows, features), F32), dma((2, 4))],
     )(*results)
 
 

time: 48.2 us -> 46.4 us (0.963)
  Pallas kernels: 47.4 us -> 45.6 us
    pallas_call x1, Pallas kernels: 45.6 us -> 43.8 us  [shards(): pl.pallas_call(functools.partial(kernel, tile_count), out_shape=(out, out...]
where the time goes in v3:
time: 46.4 us; the launch traced here: 46.2 us
  Pallas kernels  45.6 us (98%)
  between operations  0.64 us (1%)
    pallas_call x1, Pallas kernels, shards(): pl.pallas_call(functools.partial(kernel, tile_count), out_shape=(out, out...  43.8 us
    pallas_call x1, Pallas kernels, shards(): pl.pallas_call(handed_on, out_shape=(out, out, out, jax.ShapeDtypeStruct(...  1.76 us

profile of v3, /device:TPU:4, one launch (start us, length us, event | category | flops | bytes accessed | tf_op | source)
XLA Modules:
  0.0 46.2 jit_solution(16318860362280735487)
XLA Ops:
  0.6 43.8 %shard_map.93 = (bf16[256,256]{1,0:T(8,128)(2,1)}, bf16[256,256]{1,0:T(8,128)(2,1)}, bf16[256,256]{1,0:T(8,128)(2,1)}, f32[8,256]{1,0:T(8,128)}) custom-call(bf16[256,256]{1,0:T(8,128)(2,1)} %q_hbm.1, bf16[256,256]{1,0:T(8,128)(2,1)} %k_hbm.1, bf16[256,256]{1,0:T(8,128)(2,1)} %v_hbm.1, bf16[256,256]{1,0:T(8,128)(2,1)} %g_hbm.1, bf16[1024,256]{1,0:T(8,128)(2,1)} %w_hbm.1, ...), custom_call_target="tpu_custom_call" | custom-call | tf_op jit(solution)/shard_map/pallas_call | solution.py:496
  44.5 1.8 %shard_map.94 = (bf16[256,256]{1,0:T(8,128)(2,1)}, bf16[256,256]{1,0:T(8,128)(2,1)}, bf16[256,256]{1,0:T(8,128)(2,1)}, f32[8,256]{1,0:T(8,128)}) custom-call(bf16[256,256]{1,0:T(8,128)(2,1)} %get-tuple-element.8.refs_0_, bf16[256,256]{1,0:T(8,128)(2,1)} %get-tuple-element.9.refs_1_, bf16[256,256]{1,0:T(8,128)(2,1)} %get-tuple-element.10.refs_2_, ...), custom_call_target="tpu_custom_call" | custom-call | tf_op jit(solution)/shard_map/pallas_call | solution.py:556

commit v4 on v3

--- a/solution.py
+++ b/solution.py
@@ -331,7 +331,7 @@
                     device_id=(x_peer(k), h),
                     device_id_type=MESH,
                 )
-                for k in range(1, nx)
+                for k in sorted(range(1, nx), key=lambda k: -min(k, nx - k))
             ]
         )
         for copy in x_copies[part]:
@@ -405,7 +405,7 @@
                     device_id=(y_peer(k), h),
                     device_id_type=MESH,
                 )
-                for k in range(1, ny)
+                for k in sorted(range(1, ny), key=lambda k: -min(k, ny - k))
             ]
         )
         for copy in y_copies[part]:
@@ -439,7 +439,7 @@
             device_id=(z_peer(k), h),
             device_id_type=MESH,
         )
-        for k in range(1, nz)
+        for k in sorted(range(1, nz), key=lambda k: -min(k, nz - k))
     ]
     for copy in z_copies:
         copy.start()

time: 46.4 us -> 45.8 us (0.987)
  the two profiles are of different devices: /device:TPU:4 before, /device:TPU:2 now
where the time goes in v4:
time: 45.8 us; the launch traced here: 45.7 us
  Pallas kernels  45 us (98%)
  between operations  0.64 us (1%)
    pallas_call x1, Pallas kernels, shards(): pl.pallas_call(functools.partial(kernel, tile_count), out_shape=(out, out...  43.3 us
    pallas_call x1, Pallas kernels, shards(): pl.pallas_call(handed_on, out_shape=(out, out, out, jax.ShapeDtypeStruct(...  1.76 us

profile of v4, /device:TPU:2, one launch (start us, length us, event | category | flops | bytes accessed | tf_op | source)
XLA Modules:
  0.0 45.7 jit_solution(17148299575081382802)
XLA Ops:
  0.6 43.3 %shard_map.93 = (bf16[256,256]{1,0:T(8,128)(2,1)}, bf16[256,256]{1,0:T(8,128)(2,1)}, bf16[256,256]{1,0:T(8,128)(2,1)}, f32[8,256]{1,0:T(8,128)}) custom-call(bf16[256,256]{1,0:T(8,128)(2,1)} %q_hbm.1, bf16[256,256]{1,0:T(8,128)(2,1)} %k_hbm.1, bf16[256,256]{1,0:T(8,128)(2,1)} %v_hbm.1, bf16[256,256]{1,0:T(8,128)(2,1)} %g_hbm.1, bf16[1024,256]{1,0:T(8,128)(2,1)} %w_hbm.1, ...), custom_call_target="tpu_custom_call" | custom-call | tf_op jit(solution)/shard_map/pallas_call | solution.py:496
  43.9 1.8 %shard_map.94 = (bf16[256,256]{1,0:T(8,128)(2,1)}, bf16[256,256]{1,0:T(8,128)(2,1)}, bf16[256,256]{1,0:T(8,128)(2,1)}, f32[8,256]{1,0:T(8,128)}) custom-call(bf16[256,256]{1,0:T(8,128)(2,1)} %get-tuple-element.8.refs_0_, bf16[256,256]{1,0:T(8,128)(2,1)} %get-tuple-element.9.refs_1_, bf16[256,256]{1,0:T(8,128)(2,1)} %get-tuple-element.10.refs_2_, ...), custom_call_target="tpu_custom_call" | custom-call | tf_op jit(solution)/shard_map/pallas_call | solution.py:556

commit v5 on v4

--- a/solution.py
+++ b/solution.py
@@ -379,9 +379,12 @@
         for n in range(5):
             part = slice(n * 128, (n + 1) * 128)
             dscore[part, cols] = (weights[part, cols] * (grad_weight[part] - delta)).astype(BF)
-    kback[...] = dot(dscore[CELLS:EXT, :], qstack[...]).astype(BF)
     key_returns = [give_back(0, kback, kreturned, side) for side in order]
-    for copy in key_returns:
+    for copy, side in zip(key_returns, order):
+        own = slice(side * STRIP, (side + 1) * STRIP)
+        kback[own, :] = dot(
+            dscore[CELLS + side * STRIP : CELLS + (side + 1) * STRIP, :], qstack[...]
+        ).astype(BF)
         copy.start()
 
     block = nz * rows

time: 45.8 us -> 45.8 us (level)
  no operation moved by 1% of the time
where the time goes in v5:
time: 45.8 us; the launch traced here: 45.7 us
  Pallas kernels  45 us (98%)
  between operations  0.64 us (1%)
    pallas_call x1, Pallas kernels, shards(): pl.pallas_call(functools.partial(kernel, tile_count), out_shape=(out, out...  43.3 us
    pallas_call x1, Pallas kernels, shards(): pl.pallas_call(handed_on, out_shape=(out, out, out, jax.ShapeDtypeStruct(...  1.76 us

profile of v5, /device:TPU:2, one launch (start us, length us, event | category | flops | bytes accessed | tf_op | source)
XLA Modules:
  0.0 45.7 jit_solution(17431772419247609286)
XLA Ops:
  0.6 43.3 %shard_map.93 = (bf16[256,256]{1,0:T(8,128)(2,1)}, bf16[256,256]{1,0:T(8,128)(2,1)}, bf16[256,256]{1,0:T(8,128)(2,1)}, f32[8,256]{1,0:T(8,128)}) custom-call(bf16[256,256]{1,0:T(8,128)(2,1)} %q_hbm.1, bf16[256,256]{1,0:T(8,128)(2,1)} %k_hbm.1, bf16[256,256]{1,0:T(8,128)(2,1)} %v_hbm.1, bf16[256,256]{1,0:T(8,128)(2,1)} %g_hbm.1, bf16[1024,256]{1,0:T(8,128)(2,1)} %w_hbm.1, ...), custom_call_target="tpu_custom_call" | custom-call | tf_op jit(solution)/shard_map/pallas_call | solution.py:499
  43.9 1.8 %shard_map.94 = (bf16[256,256]{1,0:T(8,128)(2,1)}, bf16[256,256]{1,0:T(8,128)(2,1)}, bf16[256,256]{1,0:T(8,128)(2,1)}, f32[8,256]{1,0:T(8,128)}) custom-call(bf16[256,256]{1,0:T(8,128)(2,1)} %get-tuple-element.8.refs_0_, bf16[256,256]{1,0:T(8,128)(2,1)} %get-tuple-element.9.refs_1_, bf16[256,256]{1,0:T(8,128)(2,1)} %get-tuple-element.10.refs_2_, ...), custom_call_target="tpu_custom_call" | custom-call | tf_op jit(solution)/shard_map/pallas_call | solution.py:559
